TPU v7x, 1024 devices: a whole 8x8x8 slice. The times are simulated.
1024 devices in a mesh: qa: 32 (over x, z_hi), qb: 32 (over y, z_lo, core).
Axes of the slice: x: 8, y: 8, z: 8 (z_hi: 4, z_lo: 2; z = z_hi * 2 + z_lo), core: 2. Of those that a mesh axis runs over, the one named last changes fastest.
Arguments:
- state: float32 [32, 32, 128, 8, 128], P('qa', 'qb'), may hold values from -6 to 6
- costate: float32 [32, 32, 128, 8, 128], P('qa', 'qb'), may hold values from -6 to 6
- gates: float32 [2, 4, 128, 128], replicated, may hold values from -0.5 to 0.5
- targets: int32 [2, 4], replicated, may hold values from 0 to 1
Outputs:
- start_state: float32 [32, 32, 128, 8, 128], P('qa', 'qb')
- start_costate: float32 [32, 32, 128, 8, 128], P('qa', 'qb')
- gate_grads: float32 [2, 4, 128, 128], replicated
Inputs may be any that keep to these rules, and one draw needn't show every extreme that they name: `targets`: 0 means the gate acts on the last index, 1 on the third from last.
All inputs are finite; a program needn't handle non-finite values.
Results may differ from a plain program's by a relative error of at most 0.0003.
Values sent between devices are 32-bit elements; how exact they have to be, the bound alone decides.
A program may use at most 64 MiB of HBM per device.

v0:
```python
import jax
import jax.numpy as jnp
from jax import lax
from jax.sharding import PartitionSpec as P


def unapply(values, matrix, target):

    def apply_low(inner):
        return jnp.einsum("abmsi,ij->abmsj", inner, matrix, precision=lax.Precision.HIGHEST)

    def apply_middle(inner):
        return jnp.einsum("abisl,ij->abjsl", inner, matrix, precision=lax.Precision.HIGHEST)

    return lax.cond(target == 0, apply_low, apply_middle, values)


def gradient(adjoint, earlier, target):

    def from_low(inner):
        return jnp.einsum("abmsi,abmsj->ij", inner[0], inner[1], precision=lax.Precision.HIGHEST)

    def from_middle(inner):
        return jnp.einsum("abisl,abjsl->ij", inner[0], inner[1], precision=lax.Precision.HIGHEST)

    return lax.cond(target == 0, from_low, from_middle, (adjoint, earlier))


def gate_step(amplitudes, adjoint, matrix, target):
    earlier = unapply(amplitudes, matrix, target)
    derivative = gradient(adjoint, earlier, target)
    return (earlier, unapply(adjoint, matrix, target), derivative)


def shards(state, costate, gates, targets):
    layout = state.shape
    rest_count = lax.axis_size("qa") * lax.axis_size("qb") * layout[2] * layout[3]
    amplitudes = state
    adjoint = costate
    pending = None
    results = [None, None]
    for block_index in (1, 0):
        derivs = [None, None, None, None]
        last_gate = 3
        for gate_index in range(last_gate, -1, -1):
            amplitudes, adjoint, derivs[gate_index] = gate_step(
                amplitudes,
                adjoint,
                gates[block_index, gate_index],
                targets[block_index, gate_index],
            )
        stacked = jnp.stack(derivs)
        stacked = lax.psum(stacked, ("qa", "qb"))
        results[block_index] = stacked
        if block_index == 1:
            amplitudes, adjoint = (
                lax.all_to_all(amplitudes, "qb", split_axis=2, concat_axis=1, tiled=True),
                lax.all_to_all(adjoint, "qb", split_axis=2, concat_axis=1, tiled=True),
            )
            amplitudes = amplitudes.reshape(layout)
            adjoint = adjoint.reshape(layout)
    amplitudes, adjoint = (
        lax.all_to_all(amplitudes, "qa", split_axis=2, concat_axis=0, tiled=True),
        lax.all_to_all(adjoint, "qa", split_axis=2, concat_axis=0, tiled=True),
    )
    amplitudes = amplitudes.reshape(layout)
    adjoint = adjoint.reshape(layout)
    whole = jnp.stack(results)
    gate_grads = whole * rest_count ** (-0.5)
    return (amplitudes, adjoint, gate_grads)


def solution(mesh):
    in_specs = (P("qa", "qb", None, None, None), P("qa", "qb", None, None, None), P(), P())
    out_specs = (P("qa", "qb", None, None, None), P("qa", "qb", None, None, None), P())
    return jax.shard_map(shards, mesh=mesh, in_specs=in_specs, out_specs=out_specs, check_vma=False)
```

profile of v0, /device:TPU:1, one launch (start us, length us, event | category | flops | bytes accessed | tf_op | source)
XLA Modules:
  0.0 423.6 jit_solution(15144099824215240158)
XLA Ops:
  7.2 1.7 fusion.110
  11.4 1.8 slice_bitcast_fusion
  13.2 1.5 conditional.32
  13.2 1.5 convolution_bitcast_fusion.16
  16.4 1.1 copy.156
  17.6 17.8 %all-to-all-start.2 = ((f32[1,1,128,8,128]{4,3,1,0,2:T(8,128)}), f32[1,1,128,8,128]{4,3,1,0,2:T(8,128)S(1)}, u32[]{:S(2)}, u32[]{:S(2)}) async-start(f32[1,1,128,8,128]{4,3,1,0,2:T(8,128)} %bitcast.433), calls=%async_computation.2 | async-start | bytes 1048576 | tf_op jit(solution)/shard_map/all_to_all | solution.py:58
  35.4 1.5 conditional.24
  35.4 1.5 convolution_bitcast_fusion
  36.9 1.4 conditional.25
  36.9 1.4 convolution_bitcast_fusion.3
  38.3 1.4 conditional.26
  38.3 1.4 convolution_bitcast_fusion.5
  39.7 2.4 conditional.27
  39.7 2.4 convolution_bitcast_fusion.7
  42.1 2.1 copy.47
  44.2 8.1 %all-to-all-done.2 = f32[1,1,128,8,128]{4,3,1,0,2:T(8,128)S(1)} async-done(((f32[1,1,128,8,128]{4,3,1,0,2:T(8,128)}), f32[1,1,128,8,128]{4,3,1,0,2:T(8,128)S(1)}, u32[]{:S(2)}, u32[]{:S(2)}) %all-to-all-start.2) | async-done | bytes 524320 | tf_op jit(solution)/shard_map/all_to_all | solution.py:58
  52.4 5.5 %all-to-all-start = ((f32[1,1,128,8,128]{4,3,1,0,2:T(8,128)}), f32[1,1,128,8,128]{4,3,1,0,2:T(8,128)}, u32[]{:S(2)}, u32[]{:S(2)}) async-start(f32[1,1,128,8,128]{4,3,1,0,2:T(8,128)} %copy.47), calls=%async_computation | async-start | bytes 1048576 | tf_op jit(solution)/shard_map/all_to_all | solution.py:57
  60.3 1.6 conditional.36
  60.5 1.4 convolution_bitcast_fusion.23
  61.9 2.4 conditional.37
  61.9 2.4 convolution_bitcast_fusion.25
  64.3 2.5 conditional.38
  64.3 2.5 convolution_bitcast_fusion.26
  66.8 2.5 conditional.39
  66.8 2.5 fusion.70
  69.3 2.2 copy.155
  71.4 3.6 all-to-all-done
  75.0 13.9 %all-to-all-start.3 = ((f32[1,1,128,8,128]{4,3,1,0,2:T(8,128)}), f32[1,1,128,8,128]{4,3,1,0,2:T(8,128)}, u32[]{:S(2)}, u32[]{:S(2)}) async-start(f32[1,1,128,8,128]{4,3,1,0,2:T(8,128)} %bitcast.434), calls=%async_computation.3 | async-start | bytes 1048576 | tf_op jit(solution)/shard_map/all_to_all | solution.py:64
  88.8 2.4 conditional.28
  88.9 2.4 convolution_bitcast_fusion.9
  91.3 2.4 conditional.29
  91.3 2.4 convolution_bitcast_fusion.11
  93.7 2.5 conditional.30
  93.7 2.5 convolution_bitcast_fusion.12
  96.1 2.5 conditional.31
  96.1 2.5 convolution_bitcast_fusion.14
  98.6 2.2 copy.54
  100.8 4.9 %all-to-all-done.3 = f32[1,1,128,8,128]{4,3,1,0,2:T(8,128)} async-done(((f32[1,1,128,8,128]{4,3,1,0,2:T(8,128)}), f32[1,1,128,8,128]{4,3,1,0,2:T(8,128)}, u32[]{:S(2)}, u32[]{:S(2)}) %all-to-all-start.3) | async-done | bytes 524320 | tf_op jit(solution)/shard_map/all_to_all | solution.py:64
  105.6 7.5 %all-to-all-start.1 = ((f32[1,1,128,8,128]{4,3,1,0,2:T(8,128)}), f32[1,1,128,8,128]{4,3,1,0,2:T(8,128)}, u32[]{:S(2)}, u32[]{:S(2)}) async-start(f32[1,1,128,8,128]{4,3,1,0,2:T(8,128)} %copy.54), calls=%async_computation.1 | async-start | bytes 1048576 | tf_op jit(solution)/shard_map/all_to_all | solution.py:63
  113.2 1.7 conditional.47
  113.2 1.6 convolution_bitcast_fusion.42
  114.9 1.2 conditional.46
  116.2 1.0 conditional.45
  117.2 1.0 conditional.44
  123.3 287.9 %all-reduce.3.cloned.1.call-done = (f32[1,4,128,128]{3,2,1,0:T(8,128)}, f32[1,4,128,128]{3,2,1,0:T(8,128)}) async-done(((f32[1,4,128,128]{3,2,1,0:T(8,128)}, f32[1,4,128,128]{3,2,1,0:T(8,128)}), (f32[1,4,128,128]{3,2,1,0:T(8,128)}, f32[1,4,128,128]{3,2,1,0:T(8,128)})) %all-reduce.3.cloned.1.call-update) | async-done | bytes 524304 | tf_op jit(solution)/shard_map/psum | solution.py:53
  411.2 1.9 maximum_multiply_fusion
  413.1 1.9 copy.209
  414.9 1.9 copy.210
  (46 shorter events, 14.5 us)
Async XLA Ops:
  11.3 1.8 copy-start.7
  13.1 1.5 copy-start.11
  17.6 17.8 %copy-start.10 = (f32[1,1,128,8,128]{4,3,2,1,0:T(8,128)S(1)}, f32[1,1,128,8,128]{4,3,2,1,0:T(8,128)}, u32[]{:S(2)}) copy-start(f32[1,1,128,8,128]{4,3,2,1,0:T(8,128)} %param.52) | copy-start | bytes 1572868
  17.6 34.8 %all-to-all-start.2 = ((f32[1,1,128,8,128]{4,3,1,0,2:T(8,128)}), f32[1,1,128,8,128]{4,3,1,0,2:T(8,128)S(1)}, u32[]{:S(2)}, u32[]{:S(2)}) async-start(f32[1,1,128,8,128]{4,3,1,0,2:T(8,128)} %bitcast.433), calls=%async_computation.2 | async-start | bytes 1048576 | tf_op jit(solution)/shard_map/all_to_all | solution.py:58
  52.4 22.6 %all-to-all-start = ((f32[1,1,128,8,128]{4,3,1,0,2:T(8,128)}), f32[1,1,128,8,128]{4,3,1,0,2:T(8,128)}, u32[]{:S(2)}, u32[]{:S(2)}) async-start(f32[1,1,128,8,128]{4,3,1,0,2:T(8,128)} %copy.47), calls=%async_computation | async-start | bytes 1048576 | tf_op jit(solution)/shard_map/all_to_all | solution.py:57
  75.0 30.7 %all-to-all-start.3 = ((f32[1,1,128,8,128]{4,3,1,0,2:T(8,128)}), f32[1,1,128,8,128]{4,3,1,0,2:T(8,128)}, u32[]{:S(2)}, u32[]{:S(2)}) async-start(f32[1,1,128,8,128]{4,3,1,0,2:T(8,128)} %bitcast.434), calls=%async_computation.3 | async-start | bytes 1048576 | tf_op jit(solution)/shard_map/all_to_all | solution.py:64
  105.6 307.4 %all-to-all-start.1 = ((f32[1,1,128,8,128]{4,3,1,0,2:T(8,128)}), f32[1,1,128,8,128]{4,3,1,0,2:T(8,128)}, u32[]{:S(2)}, u32[]{:S(2)}) async-start(f32[1,1,128,8,128]{4,3,1,0,2:T(8,128)} %copy.54), calls=%async_computation.1 | async-start | bytes 1048576 | tf_op jit(solution)/shard_map/all_to_all | solution.py:63
  113.2 298.0 %all-reduce.3.cloned.1.call-start = ((), (), s32[]{:S(2)}) async-start(), calls=%async_computation.4 | async-start | bytes 1048576 | tf_op jit(solution)/shard_map/psum | solution.py:53
  114.9 1.3 copy-start
  116.1 1.0 copy-start.8
  117.2 1.0 copy-start.4
  118.2 1.0 copy-start.1
  118.2 1.2 copy-start.5
  119.4 1.0 copy-start.2
  119.4 1.2 copy-start.6
  120.6 1.0 copy-start.3
  120.6 1.2 copy-start.9
Sparse Core Ops, SparseCore 0:
  123.4 287.7 all-reduce.2
where the time goes:
time: 425 us; the launch traced here: 424 us
  waiting for transfers between devices  304 us (72%)
  starting transfers between devices  44.7 us (11%)
  matrix products  35.7 us (8%)
  between operations  19.1 us (4%)
  local copies, waits for them, and re-layouts  16.1 us (4%)
    psum x1, waiting for transfers between devices, shards(): stacked = lax.psum(stacked, ('qa', 'qb'))  288 us
    all_to_all x1, starting transfers between devices, shards(): lax.all_to_all(adjoint, 'qb', split_axis=2, concat_axis=1, tiled=True)  17.8 us
    dot_general x10, matrix products, apply_low(): jnp.einsum('abmsi,ij->abmsj', inner, matrix, precision=lax.Precision.HIGH...  15.4 us
    all_to_all x1, starting transfers between devices, shards(): lax.all_to_all(adjoint, 'qa', split_axis=2, concat_axis=0, tiled=True)  13.9 us
    dot_general x6, matrix products, apply_middle(): jnp.einsum('abisl,ij->abjsl', inner, matrix, precision=lax.Precision.HIGH...  12.9 us
  transfers between devices with their start and end apart: 5, of which 4 were waited for; matrix products, arithmetic and copies ran while one was open for 10% of the time, Pallas kernels for 0%

commit v1 on v0

v1 whole, which is shorter than its diff:
```python
import functools

import jax
import jax.numpy as jnp
from jax import lax
from jax.experimental import pallas as pl
from jax.experimental.pallas import tpu as pltpu
from jax.sharding import PartitionSpec as P

F32 = jnp.float32
BF16 = jnp.bfloat16
HIGHEST = lax.Precision.HIGHEST
MESH = pl.DeviceIdType.MESH

CORES = 2
Z_HI = 4
CHUNK = 2


def split(value):
    high = value.astype(BF16)
    return high, (value - high.astype(F32)).astype(BF16)


def mul(left, right):
    return jnp.dot(left, right, preferred_element_type=F32)


def exact(left, right, left_dim=1, right_dim=0):
    return lax.dot_general(
        left, right, (((left_dim,), (right_dim,)), ((), ())), precision=HIGHEST, preferred_element_type=F32
    )


def main_kernel(
    cfg,
    targets,
    state,
    costate,
    gates,
    fin,
    total,
    send_b,
    recv_b,
    send_a,
    p_low,
    p_mid,
    q_pair,
    c_old,
    c_new,
    c_other,
    f_dup,
    f_low,
    f_adj,
    grads,
    raw,
    half_in,
    half,
    row_in,
    x_in,
    z_in,
    swap_send,
    swap_recv,
    own_sem,
    red_send,
    red_recv,
):
    NA, NB, ZH, C, SC, G, S, scale = cfg
    NC = S // SC
    X, J = NA // ZH, NB // C
    RB, RA = G // NB * SC, G // NA * SC
    a, b = lax.axis_index("qa"), lax.axis_index("qb")
    x, zh = a // ZH, a % ZH
    j, core = b // C, b % C

    barrier = pltpu.get_barrier_semaphore()

    def greet_b(k, carry):
        pl.semaphore_signal(barrier, inc=1, device_id=(a, (b + k) % NB), device_id_type=MESH)
        return carry

    def greet_a(k, carry):
        pl.semaphore_signal(barrier, inc=1, device_id=((a + k) % NA, b), device_id_type=MESH)
        return carry

    lax.fori_loop(1, NB, greet_b, 0)
    lax.fori_loop(1, NA, greet_a, 0)

    def products(block):
        eye_r = lax.broadcasted_iota(jnp.int32, (G, G), 0)
        eye_c = lax.broadcasted_iota(jnp.int32, (G, G), 1)
        prods = [(eye_r == eye_c).astype(F32)] * 2
        for step, g in enumerate((3, 2, 1, 0)):
            low = jnp.full((G, G), targets[block, g], jnp.int32) == 0
            mine = jnp.where(low, prods[0], prods[1])
            other = jnp.where(low, prods[1], prods[0])
            gate = gates[block * 4 + g]
            new = gate if step == 0 else exact(mine, gate)
            c_old[block, g] = mine
            c_new[block, g] = new * scale
            c_other[block, g] = other
            prods = [jnp.where(low, new, prods[0]), jnp.where(low, prods[1], new)]
        high, low_ = split(prods[0])
        p_low[block, :G, :G] = high
        p_low[block, :G, G:] = low_
        p_low[block, G:, :G] = high
        p_low[block, G:, G:] = jnp.zeros((G, G), BF16)
        high, low_ = split(prods[1].T)
        p_mid[block, :, :G] = high
        p_mid[block, :, G:] = low_

    def metrics(block):
        for g in range(4):
            other = c_other[block, g]
            high, low_ = split(exact(other, other, 1, 1))
            q_pair[block, g, :, :G] = high
            q_pair[block, g, :, G:] = low_

    def load_first(c, arr, s):
        ref = costate if arr else state
        return ref[pl.ds(c * SC + s, G, stride=S), :]

    def load_second(c, arr, s):
        return recv_b[c, arr, pl.ds(s, G, stride=SC), :]

    def transform(block, c, load, out):
        rows = jnp.concatenate([load(c, arr, s) for arr in range(2) for s in range(SC)], axis=0)
        high, low_ = split(rows)
        both = mul(jnp.concatenate([high, low_], axis=1), p_low[block])
        mid = both[:, :G] + both[:, G:]
        for arr in range(2):
            wide = jnp.concatenate([mid[(arr * SC + s) * G : (arr * SC + s + 1) * G] for s in range(SC)], axis=1)
            high, low_ = split(wide)
            done = mul(p_mid[block], jnp.concatenate([high, high], axis=0)) + mul(p_mid[block, :, :G], low_)
            for s in range(SC):
                out[c, arr, pl.ds(s, G, stride=SC), :] = done[:, s * G : (s + 1) * G]

    def derive(block, c, load):
        amps = [load(c, 0, s) for s in range(SC)]
        adjs = [load(c, 1, s) for s in range(SC)]
        for t in range(2):
            high, low_ = split(jnp.concatenate([v.T if t else v for v in amps], axis=1))
            f_dup[t, :G] = high
            f_dup[t, G:] = high
            f_low[t] = low_
            high, low_ = split(jnp.concatenate([v if t else v.T for v in adjs], axis=1))
            f_adj[t, :G] = high
            f_adj[t, G:] = low_
        for g in range(4):
            t = targets[block, g]
            wide = mul(q_pair[block, g], f_dup[t]) + mul(q_pair[block, g, :, :G], f_low[t])
            tall = jnp.concatenate([wide[:, s * G : (s + 1) * G] for s in range(SC)], axis=0)
            high, low_ = split(tall)
            quad = mul(f_adj[t], jnp.concatenate([high, low_], axis=1))
            grads[block, g] = grads[block, g] + (quad[:G, :G] + (quad[:G, G:] + quad[G:, :G]))

    def finish(block):
        per = raw.shape[2]
        for g in range(4):
            value = exact(c_old[block, g].T, exact(grads[block, g], c_new[block, g]))
            if G >= per:
                count = G // per
                raw[block, g * count : (g + 1) * count] = value.reshape(count, per, G)

    def spread(i, count):
        odd = i % 2
        return odd * ((i + 1) // 2) + (1 - odd) * (count - i // 2)

    def send_swap(c, which):
        src, dst, rows, n = (send_b, recv_b, RB, NB) if which == 0 else (send_a, fin, RA, NA)
        me = b if which == 0 else a
        mine = pl.ds(pl.multiple_of(me * rows, rows), rows)

        def one(i, carry):
            peer = (me + spread(i, n)) % n
            where = (a, peer) if which == 0 else (peer, b)
            pltpu.make_async_remote_copy(
                src_ref=src.at[c, :, pl.ds(pl.multiple_of(peer * rows, rows), rows), :],
                dst_ref=dst.at[c, :, mine, :],
                send_sem=swap_send.at[which, c],
                recv_sem=swap_recv.at[which, c],
                device_id=where,
                device_id_type=MESH,
            ).start()
            return carry

        lax.fori_loop(1, n, one, 0)
        pltpu.make_async_copy(src.at[c, :, mine, :], dst.at[c, :, mine, :], own_sem.at[which, c]).start()

    def wait_swap(c, which, sends):
        src, dst, rows, n = (send_b, recv_b, RB, NB) if which == 0 else (send_a, fin, RA, NA)
        me = b if which == 0 else a
        most = pl.ds(0, (n - 1) * rows)
        if sends:
            part = src.at[c, :, most, :]
            pltpu.make_async_copy(part, part, swap_send.at[which, c]).wait()
        else:
            part = dst.at[c, :, most, :]
            pltpu.make_async_copy(part, part, swap_recv.at[which, c]).wait()
            mine = pl.ds(pl.multiple_of(me * rows, rows), rows)
            pltpu.make_async_copy(src.at[c, :, mine, :], dst.at[c, :, mine, :], own_sem.at[which, c]).wait()

    def remote(src, dst, block, phase, where):
        return pltpu.make_async_remote_copy(
            src_ref=src,
            dst_ref=dst,
            send_sem=red_send.at[block, phase],
            recv_sem=red_recv.at[block, phase],
            device_id=where,
            device_id_type=MESH,
        )

    def took(ref, sems, block, phase):
        pltpu.make_async_copy(ref, ref, sems.at[block, phase]).wait()

    partner = (a, j * C + (1 - core))

    def reduce_core(block):
        remote(raw.at[block, pl.ds((1 - core) * J, J)], half_in.at[block], block, 0, partner).start()

    def reduce_rows(block):
        took(half_in.at[block], red_recv, block, 0)
        half[block] = raw[block, pl.ds(core * J, J)] + half_in[block]

        def one(k, carry):
            to = (j + k) % J
            remote(half.at[block, to], row_in.at[block, j], block, 1, (a, to * C + core)).start()
            return carry

        lax.fori_loop(1, J, one, 0)
        row_in[block, j] = half[block, j]

    def summed(ref, block, count):
        value = ref[block, 0]
        for i in range(1, count):
            value = value + ref[block, i]
        return value

    def reduce_x(block):
        took(row_in.at[block, pl.ds(0, J - 1)], red_recv, block, 1)
        x_in[block, x] = summed(row_in, block, J)

        def one(k, carry):
            remote(x_in.at[block, x], x_in.at[block, x], block, 2, ((x + k) % X * ZH + zh, b)).start()
            return carry

        lax.fori_loop(1, X, one, 0)

    def reduce_z(block):
        took(x_in.at[block, pl.ds(0, X - 1)], red_recv, block, 2)
        z_in[block, zh] = summed(x_in, block, X)

        def one(k, carry):
            remote(z_in.at[block, zh], z_in.at[block, zh], block, 3, (x * ZH + (zh + k) % ZH, b)).start()
            return carry

        lax.fori_loop(1, ZH, one, 0)

    def gather_rows(block):
        took(z_in.at[block, pl.ds(0, ZH - 1)], red_recv, block, 3)
        slot = core * J + j
        total[block, slot] = summed(z_in, block, ZH)

        def one(k, carry):
            to = (j + k) % J
            remote(total.at[block, slot], total.at[block, slot], block, 4, (a, to * C + core)).start()
            return carry

        lax.fori_loop(1, J, one, 0)

    def gather_core(block):
        took(total.at[block, pl.ds(0, J - 1)], red_recv, block, 4)
        part = total.at[block, pl.ds(core * J, J)]
        remote(part, part, block, 5, partner).start()

    def gather_done(block):
        took(half_in.at[block], red_recv, block, 5)

    grads[...] = jnp.zeros_like(grads)
    products(1)
    pl.semaphore_wait(barrier, NA + NB - 2)

    def first(c, carry):
        transform(1, c, load_first, send_b)
        send_swap(c, 0)
        return carry

    lax.fori_loop(0, NC, first, 0)
    metrics(1)

    def first_derive(c, carry):
        derive(1, c, load_first)
        return carry

    lax.fori_loop(0, NC, first_derive, 0)
    finish(1)
    reduce_core(1)
    products(0)
    metrics(0)
    reduce_rows(1)

    def second(c, carry):
        wait_swap(c, 0, False)
        transform(0, c, load_second, send_a)
        send_swap(c, 1)
        derive(0, c, load_second)
        return carry

    lax.fori_loop(0, NC, second, 0)
    finish(0)
    reduce_core(0)
    reduce_x(1)
    reduce_rows(0)
    reduce_z(1)
    reduce_x(0)
    gather_rows(1)
    reduce_z(0)
    gather_core(1)
    gather_rows(0)
    gather_done(1)
    gather_core(0)
    gather_done(0)

    def ending(c, carry):
        wait_swap(c, 1, False)
        wait_swap(c, 0, True)
        wait_swap(c, 1, True)
        return carry

    lax.fori_loop(0, NC, ending, 0)
    for block in range(2):
        took(half_in.at[block], red_send, block, 0)
        took(row_in.at[block, pl.ds(0, J - 1)], red_send, block, 1)
        took(x_in.at[block, pl.ds(0, X - 1)], red_send, block, 2)
        took(z_in.at[block, pl.ds(0, ZH - 1)], red_send, block, 3)
        took(total.at[block, pl.ds(0, J - 1)], red_send, block, 4)
        took(half_in.at[block], red_send, block, 5)


def layout_kernel(cfg, fin, total, out_state, out_costate, out_grads):
    NA, NB, ZH, C, SC, G, S, scale = cfg
    for arr, out in ((0, out_state), (1, out_costate)):
        for c in range(S // SC):
            for s in range(SC):
                out[pl.ds(c * SC + s, G, stride=S), :] = fin[c, arr, pl.ds(s, G, stride=SC), :]
    out_grads[...] = total[...]


def shards(zh, cores, state, costate, gates, targets):
    NA, NB = lax.axis_size("qa"), lax.axis_size("qb")
    layout = state.shape
    G, S, L = layout[2:]
    SC = CHUNK
    NC = S // SC
    X, J = NA // zh, NB // cores
    scale = float(NA * NB * G * S) ** -0.5
    cfg = (NA, NB, zh, cores, SC, G, S, scale)
    per = 4 * G // NB
    vmem = pl.BlockSpec(memory_space=pltpu.VMEM)
    fin, total = pl.pallas_call(
        functools.partial(main_kernel, cfg),
        out_shape=(
            jax.ShapeDtypeStruct((NC, 2, G * SC, L), F32),
            jax.ShapeDtypeStruct((2, NB, per, L), F32),
        ),
        in_specs=[pl.BlockSpec(memory_space=pltpu.SMEM), vmem, vmem, vmem],
        out_specs=(vmem, vmem),
        scratch_shapes=[
            pltpu.VMEM((NC, 2, G * SC, L), F32),
            pltpu.VMEM((NC, 2, G * SC, L), F32),
            pltpu.VMEM((NC, 2, G * SC, L), F32),
            pltpu.VMEM((2, 2 * G, 2 * G), BF16),
            pltpu.VMEM((2, G, 2 * G), BF16),
            pltpu.VMEM((2, 4, G, 2 * G), BF16),
            pltpu.VMEM((2, 4, G, G), F32),
            pltpu.VMEM((2, 4, G, G), F32),
            pltpu.VMEM((2, 4, G, G), F32),
            pltpu.VMEM((2, 2 * G, SC * G), BF16),
            pltpu.VMEM((2, G, SC * G), BF16),
            pltpu.VMEM((2, 2 * G, SC * G), BF16),
            pltpu.VMEM((2, 4, G, G), F32),
            pltpu.VMEM((2, NB, per, L), F32),
            pltpu.VMEM((2, J, per, L), F32),
            pltpu.VMEM((2, J, per, L), F32),
            pltpu.VMEM((2, J, per, L), F32),
            pltpu.VMEM((2, X, per, L), F32),
            pltpu.VMEM((2, zh, per, L), F32),
            pltpu.SemaphoreType.DMA((2, NC)),
            pltpu.SemaphoreType.DMA((2, NC)),
            pltpu.SemaphoreType.DMA((2, NC)),
            pltpu.SemaphoreType.DMA((2, 6)),
            pltpu.SemaphoreType.DMA((2, 6)),
        ],
        compiler_params=pltpu.CompilerParams(collective_id=0, has_side_effects=True),
        name="adjoint_main",
    )(targets, state.reshape(G * S, L), costate.reshape(G * S, L), gates.reshape(8, G, G))
    out_state, out_costate, grads = pl.pallas_call(
        functools.partial(layout_kernel, cfg),
        out_shape=(
            jax.ShapeDtypeStruct((G * S, L), F32),
            jax.ShapeDtypeStruct((G * S, L), F32),
            jax.ShapeDtypeStruct((2, NB, per, L), F32),
        ),
        in_specs=[vmem, vmem],
        out_specs=(vmem, vmem, vmem),
        name="adjoint_layout",
    )(fin, total)
    return out_state.reshape(layout), out_costate.reshape(layout), grads.reshape(2, 4, G, G)


def build(mesh, zh, cores):
    in_specs = (P("qa", "qb", None, None, None), P("qa", "qb", None, None, None), P(), P())
    out_specs = (P("qa", "qb", None, None, None), P("qa", "qb", None, None, None), P())
    return jax.shard_map(
        functools.partial(shards, zh, cores), mesh=mesh, in_specs=in_specs, out_specs=out_specs, check_vma=False
    )


def solution(mesh):
    return build(mesh, Z_HI, CORES)
```

time: 425 us -> 94.3 us (0.22)
  waiting for transfers between devices: 304 us -> 0 us
  Pallas kernels: 0 us -> 93.5 us
  starting transfers between devices: 44.7 us -> 0 us
  matrix products: 35.7 us -> 0 us
  between operations: 19.1 us -> 0.64 us
  local copies, waits for them, and re-layouts: 16.1 us -> 0 us
    psum x1 -> x0, waiting for transfers between devices: 288 us -> none  [shards(): stacked = lax.psum(stacked, ('qa', 'qb'))]
    pallas_call x0 -> x2, Pallas kernels: none -> 93.5 us  [the longest x1 90.7 us: shards(): pl.pallas_call(functools.partial(main_kernel, cfg), out_shape=(jax.ShapeD...]
    all_to_all x4 -> x0, starting transfers between devices: 44.7 us -> none  [the longest x1 17.8 us: shards(): lax.all_to_all(adjoint, 'qb', split_axis=2, concat_axis=1, tiled=True)]
    dot_general x24 -> x0, matrix products: 35.7 us -> none  [the longest x10 15.4 us: apply_low(): jnp.einsum('abmsi,ij->abmsj', inner, matrix, precision=lax.Precision.HIGH...]
    all_to_all x4 -> x0, waiting for transfers between devices: 16.6 us -> none  [the longest x1 8.14 us: shards(): lax.all_to_all(adjoint, 'qb', split_axis=2, concat_axis=1, tiled=True)]
    cond x4 -> x0, local copies, waits for them, and re-layouts: 7.58 us -> none  [unapply(): return lax.cond(target == 0, apply_low, apply_middle, values)]
    unnamed x26 -> x0, local copies, waits for them, and re-layouts: 4.87 us -> none
  transfers between devices with their start and end apart: 5 -> 0, of which waited for: 4 -> 0; matrix products, arithmetic and copies ran while one was open for 10% -> 0% of each run, Pallas kernels for 0% -> 0%
where the time goes in v1:
time: 94.3 us; the launch traced here: 94.1 us
  Pallas kernels  93.5 us (99%)
    pallas_call x1, Pallas kernels, shards(): pl.pallas_call(functools.partial(main_kernel, cfg), out_shape=(jax.ShapeD...  90.7 us
    pallas_call x1, Pallas kernels, shards(): pl.pallas_call(functools.partial(layout_kernel, cfg), out_shape=(jax.Shap...  2.76 us

profile of v1, /device:TPU:1, one launch (start us, length us, event | category | flops | bytes accessed | tf_op | source)
XLA Modules:
  0.0 94.1 jit_solution(11342857231768362075)
XLA Ops:
  0.6 90.7 %adjoint_main.1 = (f32[4,2,256,128]{3,2,1,0:T(8,128)}, f32[2,32,16,128]{3,2,1,0:T(8,128)}) custom-call(s32[2,4]{1,0:T(2,128)} %targets.1, f32[1024,128]{1,0:T(8,128)} %bitcast.6, f32[1024,128]{1,0:T(8,128)} %bitcast.7, f32[8,128,128]{2,1,0:T(8,128)} %bitcast.8), custom_call_target="tpu_custom_call" | custom-call | tf_op jit(solution)/shard_map/adjoint_main/pallas_call | solution.py:360
  91.3 2.8 %adjoint_layout.1 = (f32[1024,128]{1,0:T(8,128)}, f32[1024,128]{1,0:T(8,128)}, f32[2,32,16,128]{3,2,1,0:T(8,128)}) custom-call(f32[4,2,256,128]{3,2,1,0:T(8,128)} %get-tuple-element.8.fin, f32[2,32,16,128]{3,2,1,0:T(8,128)} %get-tuple-element.9.total), custom_call_target="tpu_custom_call" | custom-call | tf_op jit(solution)/shard_map/adjoint_layout/pallas_call | solution.py:397

commit v2 on v1

--- a/solution.py
+++ b/solution.py
@@ -39,6 +39,7 @@
     costate,
     gates,
     fin,
+    total_lo,
     total,
     send_b,
     recv_b,
@@ -46,24 +47,30 @@
     p_low,
     p_mid,
     q_pair,
-    c_old,
-    c_new,
+    o_pair,
+    n_dup,
+    n_low,
     c_other,
     f_dup,
     f_low,
     f_adj,
     grads,
     raw,
+    raw_lo,
     half_in,
     half,
     row_in,
     x_in,
     z_in,
+    part_in,
+    share_in,
     swap_send,
     swap_recv,
     own_sem,
     red_send,
     red_recv,
+    low_send,
+    low_recv,
 ):
     NA, NB, ZH, C, SC, G, S, scale = cfg
     NC = S // SC
@@ -96,8 +103,13 @@
             other = jnp.where(low, prods[1], prods[0])
             gate = gates[block * 4 + g]
             new = gate if step == 0 else exact(mine, gate)
-            c_old[block, g] = mine
-            c_new[block, g] = new * scale
+            high, low_ = split(mine.T)
+            o_pair[block, g, :, :G] = high
+            o_pair[block, g, :, G:] = low_
+            high, low_ = split(new * scale)
+            n_dup[block, g, :G] = high
+            n_dup[block, g, G:] = high
+            n_low[block, g] = low_
             c_other[block, g] = other
             prods = [jnp.where(low, new, prods[0]), jnp.where(low, prods[1], new)]
         high, low_ = split(prods[0])
@@ -135,7 +147,7 @@
             for s in range(SC):
                 out[c, arr, pl.ds(s, G, stride=SC), :] = done[:, s * G : (s + 1) * G]
 
-    def derive(block, c, load):
+    def prepare(c, load):
         amps = [load(c, 0, s) for s in range(SC)]
         adjs = [load(c, 1, s) for s in range(SC)]
         for t in range(2):
@@ -146,7 +158,9 @@
             high, low_ = split(jnp.concatenate([v if t else v.T for v in adjs], axis=1))
             f_adj[t, :G] = high
             f_adj[t, G:] = low_
-        for g in range(4):
+
+    def derive(block, chosen):
+        for g in chosen:
             t = targets[block, g]
             wide = mul(q_pair[block, g], f_dup[t]) + mul(q_pair[block, g, :, :G], f_low[t])
             tall = jnp.concatenate([wide[:, s * G : (s + 1) * G] for s in range(SC)], axis=0)
@@ -154,13 +168,11 @@
             quad = mul(f_adj[t], jnp.concatenate([high, low_], axis=1))
             grads[block, g] = grads[block, g] + (quad[:G, :G] + (quad[:G, G:] + quad[G:, :G]))
 
-    def finish(block):
-        per = raw.shape[2]
-        for g in range(4):
-            value = exact(c_old[block, g].T, exact(grads[block, g], c_new[block, g]))
-            if G >= per:
-                count = G // per
-                raw[block, g * count : (g + 1) * count] = value.reshape(count, per, G)
+    def finished(block, g):
+        high, low_ = split(grads[block, g])
+        part = mul(jnp.concatenate([high, low_], axis=1), n_dup[block, g]) + mul(high, n_low[block, g])
+        high, low_ = split(part)
+        return mul(o_pair[block, g], jnp.concatenate([high, high], axis=0)) + mul(o_pair[block, g, :, :G], low_)
 
     def spread(i, count):
         odd = i % 2
@@ -200,126 +212,171 @@
             mine = pl.ds(pl.multiple_of(me * rows, rows), rows)
             pltpu.make_async_copy(src.at[c, :, mine, :], dst.at[c, :, mine, :], own_sem.at[which, c]).wait()
 
-    def remote(src, dst, block, phase, where):
+    def remote(src, dst, send_sem, recv_sem, where):
         return pltpu.make_async_remote_copy(
-            src_ref=src,
-            dst_ref=dst,
-            send_sem=red_send.at[block, phase],
-            recv_sem=red_recv.at[block, phase],
-            device_id=where,
-            device_id_type=MESH,
+            src_ref=src, dst_ref=dst, send_sem=send_sem, recv_sem=recv_sem, device_id=where, device_id_type=MESH
         )
 
-    def took(ref, sems, block, phase):
-        pltpu.make_async_copy(ref, ref, sems.at[block, phase]).wait()
+    def took(ref, sem):
+        pltpu.make_async_copy(ref, ref, sem).wait()
+
+    def summed(ref, count):
+        value = ref[0]
+        for i in range(1, count):
+            value = value + ref[i]
+        return value
 
     partner = (a, j * C + (1 - core))
 
-    def reduce_core(block):
-        remote(raw.at[block, pl.ds((1 - core) * J, J)], half_in.at[block], block, 0, partner).start()
-
-    def reduce_rows(block):
-        took(half_in.at[block], red_recv, block, 0)
-        half[block] = raw[block, pl.ds(core * J, J)] + half_in[block]
+    def reduce_core():
+        remote(raw.at[pl.ds((1 - core) * J, J)], half_in, red_send.at[0], red_recv.at[0], partner).start()
+
+    def reduce_rows():
+        took(half_in, red_recv.at[0])
+        half[...] = raw[pl.ds(core * J, J)] + half_in[...]
 
         def one(k, carry):
             to = (j + k) % J
-            remote(half.at[block, to], row_in.at[block, j], block, 1, (a, to * C + core)).start()
+            remote(half.at[to], row_in.at[j], red_send.at[1], red_recv.at[1], (a, to * C + core)).start()
             return carry
 
         lax.fori_loop(1, J, one, 0)
-        row_in[block, j] = half[block, j]
-
-    def summed(ref, block, count):
-        value = ref[block, 0]
-        for i in range(1, count):
-            value = value + ref[block, i]
-        return value
-
-    def reduce_x(block):
-        took(row_in.at[block, pl.ds(0, J - 1)], red_recv, block, 1)
-        x_in[block, x] = summed(row_in, block, J)
+        row_in[j] = half[j]
+
+    def reduce_x():
+        took(row_in.at[pl.ds(0, J - 1)], red_recv.at[1])
+        x_in[x] = summed(row_in, J)
 
         def one(k, carry):
-            remote(x_in.at[block, x], x_in.at[block, x], block, 2, ((x + k) % X * ZH + zh, b)).start()
+            to = ((x + k) % X * ZH + zh, b)
+            remote(x_in.at[x], x_in.at[x], red_send.at[2], red_recv.at[2], to).start()
             return carry
 
         lax.fori_loop(1, X, one, 0)
 
-    def reduce_z(block):
-        took(x_in.at[block, pl.ds(0, X - 1)], red_recv, block, 2)
-        z_in[block, zh] = summed(x_in, block, X)
+    def reduce_z():
+        took(x_in.at[pl.ds(0, X - 1)], red_recv.at[2])
+        z_in[zh] = summed(x_in, X)
 
         def one(k, carry):
-            remote(z_in.at[block, zh], z_in.at[block, zh], block, 3, (x * ZH + (zh + k) % ZH, b)).start()
+            to = (x * ZH + (zh + k) % ZH, b)
+            remote(z_in.at[zh], z_in.at[zh], red_send.at[3], red_recv.at[3], to).start()
             return carry
 
         lax.fori_loop(1, ZH, one, 0)
 
-    def gather_rows(block):
-        took(z_in.at[block, pl.ds(0, ZH - 1)], red_recv, block, 3)
+    def gather_rows():
+        took(z_in.at[pl.ds(0, ZH - 1)], red_recv.at[3])
         slot = core * J + j
-        total[block, slot] = summed(z_in, block, ZH)
+        total[slot] = summed(z_in, ZH)
 
         def one(k, carry):
             to = (j + k) % J
-            remote(total.at[block, slot], total.at[block, slot], block, 4, (a, to * C + core)).start()
+            remote(total.at[slot], total.at[slot], red_send.at[4], red_recv.at[4], (a, to * C + core)).start()
             return carry
 
         lax.fori_loop(1, J, one, 0)
 
-    def gather_core(block):
-        took(total.at[block, pl.ds(0, J - 1)], red_recv, block, 4)
-        part = total.at[block, pl.ds(core * J, J)]
-        remote(part, part, block, 5, partner).start()
-
-    def gather_done(block):
-        took(half_in.at[block], red_recv, block, 5)
+    def gather_core():
+        took(total.at[pl.ds(0, J - 1)], red_recv.at[4])
+        part = total.at[pl.ds(core * J, J)]
+        remote(part, part, red_send.at[5], red_recv.at[5], partner).start()
+
+    def gather_done():
+        took(half_in, red_recv.at[5])
+
+    def low_scatter(q):
+        def one(i, carry):
+            to = (b + spread(i, NB)) % NB
+            remote(raw_lo.at[q, to], part_in.at[q, b], low_send.at[q, 0], low_recv.at[q, 0], (a, to)).start()
+            return carry
+
+        lax.fori_loop(1, NB, one, 0)
+        part_in[q, b] = raw_lo[q, b]
+
+    def low_share(q):
+        took(part_in.at[q, pl.ds(0, NB - 1)], low_recv.at[q, 0])
+        share_in[q, a] = summed(part_in.at[q], NB)
+
+        def one(i, carry):
+            to = ((a + spread(i, NA)) % NA, b)
+            remote(share_in.at[q, a], share_in.at[q, a], low_send.at[q, 1], low_recv.at[q, 1], to).start()
+            return carry
+
+        lax.fori_loop(1, NA, one, 0)
+
+    def low_gather(q):
+        took(share_in.at[q, pl.ds(0, NA - 1)], low_recv.at[q, 1])
+        total_lo[q, b] = summed(share_in.at[q], NA)
+
+        def one(i, carry):
+            to = (a, (b + spread(i, NB)) % NB)
+            remote(total_lo.at[q, b], total_lo.at[q, b], low_send.at[q, 2], low_recv.at[q, 2], to).start()
+            return carry
+
+        lax.fori_loop(1, NB, one, 0)
+
+    def low_done(q):
+        took(total_lo.at[q, pl.ds(0, NB - 1)], low_recv.at[q, 2])
 
     grads[...] = jnp.zeros_like(grads)
     products(1)
+    transform(1, 0, load_first, send_b)
     pl.semaphore_wait(barrier, NA + NB - 2)
+    send_swap(0, 0)
 
     def first(c, carry):
         transform(1, c, load_first, send_b)
         send_swap(c, 0)
         return carry
 
-    lax.fori_loop(0, NC, first, 0)
+    lax.fori_loop(1, NC, first, 0)
     metrics(1)
 
     def first_derive(c, carry):
-        derive(1, c, load_first)
+        prepare(c, load_first)
+        derive(1, range(4))
         return carry
 
     lax.fori_loop(0, NC, first_derive, 0)
-    finish(1)
-    reduce_core(1)
+    per = raw.shape[1]
+    for g in range(4):
+        raw[g * G // per : (g + 1) * G // per] = finished(1, g).reshape(G // per, per, G)
+    reduce_core()
     products(0)
     metrics(0)
-    reduce_rows(1)
+    reduce_rows()
 
     def second(c, carry):
         wait_swap(c, 0, False)
         transform(0, c, load_second, send_a)
         send_swap(c, 1)
-        derive(0, c, load_second)
-        return carry
-
-    lax.fori_loop(0, NC, second, 0)
-    finish(0)
-    reduce_core(0)
-    reduce_x(1)
-    reduce_rows(0)
-    reduce_z(1)
-    reduce_x(0)
-    gather_rows(1)
-    reduce_z(0)
-    gather_core(1)
-    gather_rows(0)
-    gather_done(1)
-    gather_core(0)
-    gather_done(0)
+        prepare(c, load_second)
+        derive(0, range(4))
+        return carry
+
+    lax.fori_loop(0, NC - 1, second, 0)
+    wait_swap(NC - 1, 0, False)
+    prepare(NC - 1, load_second)
+    per = raw_lo.shape[2]
+    for q in range(2):
+        derive(0, (2 * q, 2 * q + 1))
+        for i in range(2):
+            raw_lo[q, i * G // per : (i + 1) * G // per] = finished(0, 2 * q + i).reshape(G // per, per, G)
+        low_scatter(q)
+    reduce_x()
+    transform(0, NC - 1, load_second, send_a)
+    send_swap(NC - 1, 1)
+    low_share(0)
+    low_share(1)
+    reduce_z()
+    gather_rows()
+    low_gather(0)
+    low_gather(1)
+    gather_core()
+    gather_done()
+    low_done(0)
+    low_done(1)
 
     def ending(c, carry):
         wait_swap(c, 1, False)
@@ -328,22 +385,26 @@
         return carry
 
     lax.fori_loop(0, NC, ending, 0)
-    for block in range(2):
-        took(half_in.at[block], red_send, block, 0)
-        took(row_in.at[block, pl.ds(0, J - 1)], red_send, block, 1)
-        took(x_in.at[block, pl.ds(0, X - 1)], red_send, block, 2)
-        took(z_in.at[block, pl.ds(0, ZH - 1)], red_send, block, 3)
-        took(total.at[block, pl.ds(0, J - 1)], red_send, block, 4)
-        took(half_in.at[block], red_send, block, 5)
-
-
-def layout_kernel(cfg, fin, total, out_state, out_costate, out_grads):
-    NA, NB, ZH, C, SC, G, S, scale = cfg
+    took(half_in, red_send.at[0])
+    took(row_in.at[pl.ds(0, J - 1)], red_send.at[1])
+    took(x_in.at[pl.ds(0, X - 1)], red_send.at[2])
+    took(z_in.at[pl.ds(0, ZH - 1)], red_send.at[3])
+    took(total.at[pl.ds(0, J - 1)], red_send.at[4])
+    took(half_in, red_send.at[5])
+    for q in range(2):
+        took(part_in.at[q, pl.ds(0, NB - 1)], low_send.at[q, 0])
+        took(share_in.at[q, pl.ds(0, NA - 1)], low_send.at[q, 1])
+        took(total_lo.at[q, pl.ds(0, NB - 1)], low_send.at[q, 2])
+
+
+def layout_kernel(S, SC, fin, total_lo, total, out_state, out_costate, out_grads):
+    rows = out_state.shape[0] // S
     for arr, out in ((0, out_state), (1, out_costate)):
         for c in range(S // SC):
             for s in range(SC):
-                out[pl.ds(c * SC + s, G, stride=S), :] = fin[c, arr, pl.ds(s, G, stride=SC), :]
-    out_grads[...] = total[...]
+                out[pl.ds(c * SC + s, rows, stride=S), :] = fin[c, arr, pl.ds(s, rows, stride=SC), :]
+    out_grads[0] = total_lo[...]
+    out_grads[1] = total[...]
 
 
 def shards(zh, cores, state, costate, gates, targets):
@@ -355,16 +416,17 @@
     X, J = NA // zh, NB // cores
     scale = float(NA * NB * G * S) ** -0.5
     cfg = (NA, NB, zh, cores, SC, G, S, scale)
-    per = 4 * G // NB
+    per, per_lo = 4 * G // NB, 2 * G // NB
     vmem = pl.BlockSpec(memory_space=pltpu.VMEM)
-    fin, total = pl.pallas_call(
+    fin, total_lo, total = pl.pallas_call(
         functools.partial(main_kernel, cfg),
         out_shape=(
             jax.ShapeDtypeStruct((NC, 2, G * SC, L), F32),
-            jax.ShapeDtypeStruct((2, NB, per, L), F32),
+            jax.ShapeDtypeStruct((2, NB, per_lo, L), F32),
+            jax.ShapeDtypeStruct((NB, per, L), F32),
         ),
         in_specs=[pl.BlockSpec(memory_space=pltpu.SMEM), vmem, vmem, vmem],
-        out_specs=(vmem, vmem),
+        out_specs=(vmem, vmem, vmem),
         scratch_shapes=[
             pltpu.VMEM((NC, 2, G * SC, L), F32),
             pltpu.VMEM((NC, 2, G * SC, L), F32),
@@ -372,39 +434,55 @@
             pltpu.VMEM((2, 2 * G, 2 * G), BF16),
             pltpu.VMEM((2, G, 2 * G), BF16),
             pltpu.VMEM((2, 4, G, 2 * G), BF16),
-            pltpu.VMEM((2, 4, G, G), F32),
-            pltpu.VMEM((2, 4, G, G), F32),
+            pltpu.VMEM((2, 4, G, 2 * G), BF16),
+            pltpu.VMEM((2, 4, 2 * G, G), BF16),
+            pltpu.VMEM((2, 4, G, G), BF16),
             pltpu.VMEM((2, 4, G, G), F32),
             pltpu.VMEM((2, 2 * G, SC * G), BF16),
             pltpu.VMEM((2, G, SC * G), BF16),
             pltpu.VMEM((2, 2 * G, SC * G), BF16),
             pltpu.VMEM((2, 4, G, G), F32),
-            pltpu.VMEM((2, NB, per, L), F32),
-            pltpu.VMEM((2, J, per, L), F32),
-            pltpu.VMEM((2, J, per, L), F32),
-            pltpu.VMEM((2, J, per, L), F32),
-            pltpu.VMEM((2, X, per, L), F32),
-            pltpu.VMEM((2, zh, per, L), F32),
+            pltpu.VMEM((NB, per, L), F32),
+            pltpu.VMEM((2, NB, per_lo, L), F32),
+            pltpu.VMEM((J, per, L), F32),
+            pltpu.VMEM((J, per, L), F32),
+            pltpu.VMEM((J, per, L), F32),
+            pltpu.VMEM((X, per, L), F32),
+            pltpu.VMEM((zh, per, L), F32),
+            pltpu.VMEM((2, NB, per_lo, L), F32),
+            pltpu.VMEM((2, NA, per_lo, L), F32),
             pltpu.SemaphoreType.DMA((2, NC)),
             pltpu.SemaphoreType.DMA((2, NC)),
             pltpu.SemaphoreType.DMA((2, NC)),
-            pltpu.SemaphoreType.DMA((2, 6)),
-            pltpu.SemaphoreType.DMA((2, 6)),
+            pltpu.SemaphoreType.DMA((6,)),
+            pltpu.SemaphoreType.DMA((6,)),
+            pltpu.SemaphoreType.DMA((2, 3)),
+            pltpu.SemaphoreType.DMA((2, 3)),
         ],
         compiler_params=pltpu.CompilerParams(collective_id=0, has_side_effects=True),
         name="adjoint_main",
     )(targets, state.reshape(G * S, L), costate.reshape(G * S, L), gates.reshape(8, G, G))
+    steps = 4
     out_state, out_costate, grads = pl.pallas_call(
-        functools.partial(layout_kernel, cfg),
+        functools.partial(layout_kernel, S, SC),
+        grid=(steps,),
         out_shape=(
             jax.ShapeDtypeStruct((G * S, L), F32),
             jax.ShapeDtypeStruct((G * S, L), F32),
-            jax.ShapeDtypeStruct((2, NB, per, L), F32),
+            jax.ShapeDtypeStruct((2, 4 * G, L), F32),
         ),
-        in_specs=[vmem, vmem],
-        out_specs=(vmem, vmem, vmem),
+        in_specs=[
+            pl.BlockSpec((NC, 2, G * SC // steps, L), lambda i: (0, 0, i, 0)),
+            pl.BlockSpec((4 * G // steps, L), lambda i: (i, 0)),
+            pl.BlockSpec((4 * G // steps, L), lambda i: (i, 0)),
+        ],
+        out_specs=(
+            pl.BlockSpec((G * S // steps, L), lambda i: (i, 0)),
+            pl.BlockSpec((G * S // steps, L), lambda i: (i, 0)),
+            pl.BlockSpec((2, 4 * G // steps, L), lambda i: (0, i, 0)),
+        ),
         name="adjoint_layout",
-    )(fin, total)
+    )(fin, total_lo.reshape(4 * G, L), total.reshape(4 * G, L))
     return out_state.reshape(layout), out_costate.reshape(layout), grads.reshape(2, 4, G, G)
 
 

time: 94.3 us -> 97.9 us (1.038)
  Pallas kernels: 93.5 us -> 97 us
    pallas_call x1, Pallas kernels: 90.7 us -> 93.5 us  [shards(): pl.pallas_call(functools.partial(main_kernel, cfg), out_shape=(jax.ShapeD...]
where the time goes in v2:
time: 97.9 us; the launch traced here: 97.6 us
  Pallas kernels  97 us (99%)
    pallas_call x1, Pallas kernels, shards(): pl.pallas_call(functools.partial(main_kernel, cfg), out_shape=(jax.ShapeD...  93.5 us
    pallas_call x1, Pallas kernels, shards(): pl.pallas_call(functools.partial(layout_kernel, S, SC), grid=(steps,), ou...  3.54 us

profile of v2, /device:TPU:1, one launch (start us, length us, event | category | flops | bytes accessed | tf_op | source)
XLA Modules:
  0.0 97.6 jit_solution(14523333412468874895)
XLA Ops:
  0.6 93.5 %adjoint_main.1 = (f32[4,2,256,128]{3,2,1,0:T(8,128)}, f32[2,32,8,128]{3,2,1,0:T(8,128)}, f32[32,16,128]{2,1,0:T(8,128)}) custom-call(s32[2,4]{1,0:T(2,128)} %targets.1, f32[1024,128]{1,0:T(8,128)} %bitcast.8, f32[1024,128]{1,0:T(8,128)} %bitcast.9, f32[8,128,128]{2,1,0:T(8,128)} %bitcast.10), custom_call_target="tpu_custom_call" | custom-call | tf_op jit(solution)/shard_map/adjoint_main/pallas_call | solution.py:421
  94.1 3.5 %adjoint_layout.1 = (f32[1024,128]{1,0:T(8,128)}, f32[1024,128]{1,0:T(8,128)}, f32[2,512,128]{2,1,0:T(8,128)}) custom-call(f32[4,2,256,128]{3,2,1,0:T(8,128)} %get-tuple-element.9.fin, f32[512,128]{1,0:T(8,128)} %bitcast.11, f32[512,128]{1,0:T(8,128)} %bitcast.12), custom_call_target="tpu_custom_call" | custom-call | tf_op jit(solution)/shard_map/adjoint_layout/pallas_call | solution.py:466

commit v3 on v1

--- a/solution.py
+++ b/solution.py
@@ -35,19 +35,24 @@
 def main_kernel(
     cfg,
     targets,
+    state_in,
+    costate_in,
+    gates_in,
+    fin,
+    total,
     state,
     costate,
     gates,
-    fin,
-    total,
+    load_sem,
     send_b,
     recv_b,
     send_a,
     p_low,
     p_mid,
     q_pair,
-    c_old,
-    c_new,
+    o_pair,
+    n_dup,
+    n_low,
     c_other,
     f_dup,
     f_low,
@@ -83,6 +88,12 @@
         pl.semaphore_signal(barrier, inc=1, device_id=((a + k) % NA, b), device_id_type=MESH)
         return carry
 
+    loads = [
+        pltpu.make_async_copy(src, dst, load_sem.at[i])
+        for i, (src, dst) in enumerate(((gates_in, gates), (state_in, state), (costate_in, costate)))
+    ]
+    for load in loads:
+        load.start()
     lax.fori_loop(1, NB, greet_b, 0)
     lax.fori_loop(1, NA, greet_a, 0)
 
@@ -96,8 +107,13 @@
             other = jnp.where(low, prods[1], prods[0])
             gate = gates[block * 4 + g]
             new = gate if step == 0 else exact(mine, gate)
-            c_old[block, g] = mine
-            c_new[block, g] = new * scale
+            high, low_ = split(mine.T)
+            o_pair[block, g, :, :G] = high
+            o_pair[block, g, :, G:] = low_
+            high, low_ = split(new * scale)
+            n_dup[block, g, :G] = high
+            n_dup[block, g, G:] = high
+            n_low[block, g] = low_
             c_other[block, g] = other
             prods = [jnp.where(low, new, prods[0]), jnp.where(low, prods[1], new)]
         high, low_ = split(prods[0])
@@ -157,10 +173,11 @@
     def finish(block):
         per = raw.shape[2]
         for g in range(4):
-            value = exact(c_old[block, g].T, exact(grads[block, g], c_new[block, g]))
-            if G >= per:
-                count = G // per
-                raw[block, g * count : (g + 1) * count] = value.reshape(count, per, G)
+            high, low_ = split(grads[block, g])
+            part = mul(jnp.concatenate([high, low_], axis=1), n_dup[block, g]) + mul(high, n_low[block, g])
+            high, low_ = split(part)
+            value = mul(o_pair[block, g], jnp.concatenate([high, high], axis=0)) + mul(o_pair[block, g, :, :G], low_)
+            raw[block, g * G // per : (g + 1) * G // per] = value.reshape(G // per, per, G)
 
     def spread(i, count):
         odd = i % 2
@@ -277,15 +294,20 @@
         took(half_in.at[block], red_recv, block, 5)
 
     grads[...] = jnp.zeros_like(grads)
+    loads[0].wait()
     products(1)
+    loads[1].wait()
+    loads[2].wait()
+    transform(1, 0, load_first, send_b)
     pl.semaphore_wait(barrier, NA + NB - 2)
+    send_swap(0, 0)
 
     def first(c, carry):
         transform(1, c, load_first, send_b)
         send_swap(c, 0)
         return carry
 
-    lax.fori_loop(0, NC, first, 0)
+    lax.fori_loop(1, NC, first, 0)
     metrics(1)
 
     def first_derive(c, carry):
@@ -363,17 +385,22 @@
             jax.ShapeDtypeStruct((NC, 2, G * SC, L), F32),
             jax.ShapeDtypeStruct((2, NB, per, L), F32),
         ),
-        in_specs=[pl.BlockSpec(memory_space=pltpu.SMEM), vmem, vmem, vmem],
+        in_specs=[pl.BlockSpec(memory_space=pltpu.SMEM)] + [pl.BlockSpec(memory_space=pltpu.HBM)] * 3,
         out_specs=(vmem, vmem),
         scratch_shapes=[
+            pltpu.VMEM((G * S, L), F32),
+            pltpu.VMEM((G * S, L), F32),
+            pltpu.VMEM((8, G, G), F32),
+            pltpu.SemaphoreType.DMA((3,)),
             pltpu.VMEM((NC, 2, G * SC, L), F32),
             pltpu.VMEM((NC, 2, G * SC, L), F32),
             pltpu.VMEM((NC, 2, G * SC, L), F32),
             pltpu.VMEM((2, 2 * G, 2 * G), BF16),
             pltpu.VMEM((2, G, 2 * G), BF16),
             pltpu.VMEM((2, 4, G, 2 * G), BF16),
-            pltpu.VMEM((2, 4, G, G), F32),
-            pltpu.VMEM((2, 4, G, G), F32),
+            pltpu.VMEM((2, 4, G, 2 * G), BF16),
+            pltpu.VMEM((2, 4, 2 * G, G), BF16),
+            pltpu.VMEM((2, 4, G, G), BF16),
             pltpu.VMEM((2, 4, G, G), F32),
             pltpu.VMEM((2, 2 * G, SC * G), BF16),
             pltpu.VMEM((2, G, SC * G), BF16),
@@ -391,7 +418,9 @@
             pltpu.SemaphoreType.DMA((2, 6)),
             pltpu.SemaphoreType.DMA((2, 6)),
         ],
-        compiler_params=pltpu.CompilerParams(collective_id=0, has_side_effects=True),
+        compiler_params=pltpu.CompilerParams(
+            collective_id=0, has_side_effects=True
+        ),
         name="adjoint_main",
     )(targets, state.reshape(G * S, L), costate.reshape(G * S, L), gates.reshape(8, G, G))
     out_state, out_costate, grads = pl.pallas_call(

time: 94.3 us -> 93.4 us (level)
  no operation moved by 1% of the time
where the time goes in v3:
time: 93.4 us; the launch traced here: 93.3 us
  Pallas kernels  92.6 us (99%)
    pallas_call x1, Pallas kernels, shards(): pl.pallas_call(functools.partial(main_kernel, cfg), out_shape=(jax.ShapeD...  89.9 us
    pallas_call x1, Pallas kernels, shards(): pl.pallas_call(functools.partial(layout_kernel, cfg), out_shape=(jax.Shap...  2.76 us

profile of v3, /device:TPU:1, one launch (start us, length us, event | category | flops | bytes accessed | tf_op | source)
XLA Modules:
  0.0 93.3 jit_solution(4107523712586421507)
XLA Ops:
  0.6 89.9 %adjoint_main.1 = (f32[4,2,256,128]{3,2,1,0:T(8,128)}, f32[2,32,16,128]{3,2,1,0:T(8,128)}) custom-call(s32[2,4]{1,0:T(2,128)} %targets.1, f32[1024,128]{1,0:T(8,128)} %bitcast.6, f32[1024,128]{1,0:T(8,128)} %bitcast.7, f32[8,128,128]{2,1,0:T(8,128)} %bitcast.8), custom_call_target="tpu_custom_call" | custom-call | tf_op jit(solution)/shard_map/adjoint_main/pallas_call | solution.py:382
  90.5 2.8 %adjoint_layout.1 = (f32[1024,128]{1,0:T(8,128)}, f32[1024,128]{1,0:T(8,128)}, f32[2,32,16,128]{3,2,1,0:T(8,128)}) custom-call(f32[4,2,256,128]{3,2,1,0:T(8,128)} %get-tuple-element.8.fin, f32[2,32,16,128]{3,2,1,0:T(8,128)} %get-tuple-element.9.total), custom_call_target="tpu_custom_call" | custom-call | tf_op jit(solution)/shard_map/adjoint_layout/pallas_call | solution.py:426
